TPU v7x, 256 devices: a whole 4x4x8 slice. The times are simulated.
256 devices in a mesh: dp: 32 (over y, z), tensor: 8 (over x, core).
Axes of the slice: x: 4, y: 4, z: 8, core: 2. Of those that a mesh axis runs over, the one named last changes fastest.
Arguments:
- queries: bfloat16 [256, 6, 8192], P('dp', None, 'tensor'), may hold values from -150 to 150
- new_keys: bfloat16 [256, 6, 1024], P('dp', None, 'tensor'), may hold values from -6 to 6
- new_values: bfloat16 [256, 6, 1024], P('dp', None, 'tensor'), may hold values from -6 to 6
- key_cache: bfloat16 [256, 256, 1024], P('dp', None, 'tensor'), may hold values from -6 to 6
- value_cache: bfloat16 [256, 256, 1024], P('dp', None, 'tensor'), may hold values from -6 to 6
- cache_lengths: int32 [256], P('dp'), may hold values from 32 to 256, as said below
- accepted: int32 [256], P('tensor'), may hold values from 1 to 6
- residual: bfloat16 [256, 6, 8192], P('tensor', None, 'dp'), may hold values from -6 to 6
- out_weight: bfloat16 [8192, 8192], P('tensor', 'dp'), may hold values from -0.0625 to 0.0625
- draft_weight: bfloat16 [8192, 8192], P('tensor', 'dp'), may hold values from -0.0625 to 0.0625
Outputs:
- verified: bfloat16 [256, 6, 8192], P('tensor', None, 'dp')
- drafted: bfloat16 [5, 256, 8192], P(None, 'tensor', 'dp')
Inputs may be any that keep to these rules, and one draw needn't show every extreme that they name: `cache_lengths`: every draw has a window with all 256 slots live.
All inputs are finite; a program needn't handle non-finite values.
Results may differ from a plain program's by a relative error of at most 0.008.
Values may be sent and summed in bfloat16 or wider, within the bound.
No kernel may reach another device: no remote copies, remote signals or barrier semaphores. Data moves between devices by JAX's collectives and lax.ppermute only.
A program may use at most 64 MiB of HBM per device.

v0:
```python
import jax
import jax.numpy as jnp
from jax import lax
from jax.sharding import PartitionSpec as P

HD = 128
STEPS = 5


def spread(block, axis):
    copies = jnp.broadcast_to(block[None], (lax.axis_size(axis),) + block.shape)
    return lax.all_to_all(copies, axis, split_axis=0, concat_axis=0, tiled=True)


def accepted_of_my_windows(accepted):
    dp_size, tensor_size = (lax.axis_size("dp"), lax.axis_size("tensor"))
    ratio = dp_size // tensor_size
    pairs = []
    for j in range(dp_size):
        for i in range(tensor_size):
            source = (ratio * i + j % ratio) * tensor_size + j // ratio
            pairs.append((source, j * tensor_size + i))
    block = lax.ppermute(accepted, ("dp", "tensor"), pairs)
    rows = accepted.shape[0] // ratio
    return lax.dynamic_slice_in_dim(block, lax.axis_index("dp") % ratio * rows, rows, 0)


def pick(rows, accepted):
    chosen = jnp.arange(rows.shape[1])[None, :] == (accepted - 1)[:, None]
    return jnp.sum(
        jnp.where(chosen[:, :, None], rows, jnp.zeros((), rows.dtype)), axis=1, dtype=rows.dtype
    )


def per_device(
    queries,
    new_keys,
    new_values,
    key_cache,
    value_cache,
    cache_lengths,
    accepted,
    residual,
    out_weight,
    draft_weight,
):
    windows_here, tokens_here, query_width = queries.shape
    cache_size = key_cache.shape[1]
    kv_here = new_keys.shape[2] // HD
    group_size = query_width // HD // kv_here
    tensor_size = lax.axis_size("tensor")
    own_accepted = accepted_of_my_windows(accepted)
    draft_columns = lax.all_gather(draft_weight, "tensor", axis=0, tiled=True)
    query_split = queries.reshape(windows_here, tokens_here, kv_here, group_size, HD)
    keys_cached = key_cache.reshape(windows_here, cache_size, kv_here, HD)
    keys_fresh = new_keys.reshape(windows_here, tokens_here, kv_here, HD)
    score_cache = jnp.einsum(
        "wtkgd,wpkd->wkgtp", query_split, keys_cached, preferred_element_type=jnp.float32
    ) * HD ** (-0.5)
    score_fresh = jnp.einsum(
        "wtkgd,wpkd->wkgtp", query_split, keys_fresh, preferred_element_type=jnp.float32
    ) * HD ** (-0.5)
    live_cache = (jnp.arange(cache_size)[None, :] < cache_lengths[:, None])[:, None, None, None, :]
    live_fresh = jnp.arange(tokens_here)[None, :] <= jnp.arange(tokens_here)[:, None]
    scores = jnp.concatenate(
        [
            jnp.where(live_cache, score_cache, -jnp.inf),
            jnp.where(live_fresh, score_fresh, -jnp.inf),
        ],
        axis=-1,
    )
    largest = jnp.max(scores, axis=-1, keepdims=True)
    powered = jnp.exp(scores - largest)
    weights = (powered / jnp.sum(powered, axis=-1, keepdims=True)).astype(jnp.bfloat16)
    values_cached = value_cache.reshape(windows_here, cache_size, kv_here, HD)
    values_fresh = new_values.reshape(windows_here, tokens_here, kv_here, HD)
    mixed_rows = jnp.einsum(
        "wkgtp,wpkd->wtkgd",
        weights[..., :cache_size],
        values_cached,
        preferred_element_type=jnp.float32,
    )
    mixed_rows = mixed_rows + jnp.einsum(
        "wkgtp,wpkd->wtkgd",
        weights[..., cache_size:],
        values_fresh,
        preferred_element_type=jnp.float32,
    )
    attended = mixed_rows.astype(jnp.bfloat16).reshape(windows_here, tokens_here, query_width)
    picked_rows = spread(pick(attended, own_accepted), "dp").reshape(-1, query_width)
    picked_part = jnp.dot(picked_rows, out_weight, preferred_element_type=jnp.float32)
    block_windows, block_tokens, block_cols = residual.shape
    shares = lax.all_to_all(
        picked_part.astype(jnp.bfloat16).reshape(tensor_size, block_windows, block_cols),
        "tensor",
        split_axis=0,
        concat_axis=0,
        tiled=True,
    )
    current = (
        pick(residual, accepted).astype(jnp.float32) + jnp.sum(shares.astype(jnp.float32), axis=0)
    ).astype(jnp.bfloat16)
    partial_out = jnp.dot(
        lax.all_gather(
            attended.reshape(windows_here * tokens_here, query_width), "dp", axis=0, tiled=True
        ),
        out_weight,
        preferred_element_type=jnp.float32,
    )
    summed = lax.psum_scatter(partial_out, "tensor", scatter_dimension=0, tiled=True)
    flat_residual = residual.reshape(block_windows * block_tokens, block_cols).astype(jnp.float32)
    verified = (
        (flat_residual + summed)
        .astype(jnp.bfloat16)
        .reshape(block_windows, block_tokens, block_cols)
    )
    columns = draft_columns.reshape(-1, block_cols, draft_columns.shape[1])
    results = []
    for draft_step in range(STEPS):
        inputs = spread(current, "dp")
        product = jnp.einsum("jwk,jkn->wn", inputs, columns, preferred_element_type=jnp.float32)
        current = jnp.tanh(2.0 * product).astype(jnp.bfloat16)
        results.append(current)
    return (verified, jnp.stack(results))


def solution(mesh):
    placed = (
        P("dp", None, "tensor"),
        P("dp", None, "tensor"),
        P("dp", None, "tensor"),
        P("dp", None, "tensor"),
        P("dp", None, "tensor"),
        P("dp"),
        P("tensor"),
        P("tensor", None, "dp"),
        P("tensor", "dp"),
        P("tensor", "dp"),
    )
    return jax.shard_map(
        per_device,
        mesh=mesh,
        in_specs=placed,
        out_specs=(P("tensor", None, "dp"), P(None, "tensor", "dp")),
        check_vma=False,
    )
```

profile of v0, /device:TPU:32, one launch (start us, length us, event | category | flops | bytes accessed | tf_op | source)
XLA Modules:
  0.0 202.9 jit_solution(7244637274583813440)
XLA Ops:
  7.2 0.7 all-gather.5.cloned.1.call-update
  8.0 1.3 collective-permute-start
  9.3 0.7 iota_compare_fusion
  10.0 1.2 fusion.35
  11.2 1.4 fusion.34
  13.1 0.9 fusion.28
  14.1 1.3 fusion.29
  15.4 0.7 copy.53
  16.1 0.9 broadcast_in_dim.104
  16.9 19.1 %all-to-all-start = ((bf16[32,8,1024]{2,1,0:T(8,128)(2,1)}), bf16[32,8,1024]{2,1,0:T(8,128)(2,1)S(1)}, u32[]{:S(2)}, u32[]{:S(2)}) async-start(bf16[32,8,1024]{2,1,0:T(8,128)(2,1)} %broadcast_in_dim.104), calls=%async_computation.1 | async-start | bytes 1048576 | tf_op jit(solution)/shard_map/all_to_all | solution.py:12
  36.1 15.0 %all-to-all-done = bf16[32,8,1024]{2,1,0:T(8,128)(2,1)S(1)} async-done(((bf16[32,8,1024]{2,1,0:T(8,128)(2,1)}), bf16[32,8,1024]{2,1,0:T(8,128)(2,1)S(1)}, u32[]{:S(2)}, u32[]{:S(2)}) %all-to-all-start) | async-done | bytes 524320 | tf_op jit(solution)/shard_map/all_to_all | solution.py:12
  51.1 1.0 convolution_convert_fusion
  52.0 3.4 %all-to-all-start.1 = ((bf16[8,32,256]{2,1,0:T(8,128)(2,1)}), bf16[8,32,256]{2,1,0:T(8,128)(2,1)S(1)}, u32[]{:S(2)}, u32[]{:S(2)}) async-start(bf16[8,32,256]{2,1,0:T(8,128)(2,1)} %bitcast.19), calls=%async_computation.2 | async-start | bytes 262144 | tf_op jit(solution)/shard_map/all_to_all | solution.py:93
  55.5 5.9 %all-to-all-done.1 = bf16[8,32,256]{2,1,0:T(8,128)(2,1)S(1)} async-done(((bf16[8,32,256]{2,1,0:T(8,128)(2,1)}), bf16[8,32,256]{2,1,0:T(8,128)(2,1)S(1)}, u32[]{:S(2)}, u32[]{:S(2)}) %all-to-all-start.1) | async-done | bytes 131104 | tf_op jit(solution)/shard_map/all_to_all | solution.py:93
  61.6 23.8 %all_to_all.35 = bf16[32,32,256]{2,1,0:T(8,128)(2,1)S(1)} all-to-all(bf16[32,32,256]{2,1,0:T(8,128)(2,1)S(1)} %broadcast_in_dim.105), channel_id=1, replica_groups=mesh['dp'=32,'tensor'=8] {'dp'}, dimensions={0} | all-to-all | bytes 1048576 | tf_op jit(solution)/shard_map/all_to_all | solution.py:12
  85.4 3.2 %bitcast_dynamic-update-slice_fusion.3 = (bf16[5,32,256]{2,1,0:T(8,128)(2,1)S(1)}, bf16[32,256]{1,0:T(8,128)(2,1)S(1)}) fusion(bf16[32,32,256]{2,1,0:T(8,128)(2,1)S(1)} %all_to_all.35, bf16[32,256,256]{2,1,0:T(8,128)(2,1)} %bitcast.131), kind=kOutput, calls=%fused_computation.55 | convolution fusion | flops 134234112 | bytes 4751360 | tf_op jit(solution)/shard_map/jwk,jkn->wn/dot_general | solution.py:121
  88.6 23.2 %all_to_all.36 = bf16[32,32,256]{2,1,0:T(8,128)(2,1)S(1)} all-to-all(bf16[32,32,256]{2,1,0:T(8,128)(2,1)S(1)} %broadcast_in_dim.106), channel_id=1, replica_groups=mesh['dp'=32,'tensor'=8] {'dp'}, dimensions={0} | all-to-all | bytes 1048576 | tf_op jit(solution)/shard_map/all_to_all | solution.py:12
  111.9 0.8 bitcast_dynamic-update-slice_fusion.2
  112.7 0.9 broadcast_in_dim.107
  113.6 5.5 %all-to-all-start.4 = ((bf16[32,32,256]{2,1,0:T(8,128)(2,1)}), bf16[32,32,256]{2,1,0:T(8,128)(2,1)S(1)}, u32[]{:S(2)}, u32[]{:S(2)}) async-start(bf16[32,32,256]{2,1,0:T(8,128)(2,1)} %broadcast_in_dim.107), calls=%async_computation.5 | async-start | bytes 1048576 | tf_op jit(solution)/shard_map/all_to_all | solution.py:12
  119.2 18.9 %all-gather.3.cloned.1.call-done = bf16[1536,1024]{1,0:T(8,128)(2,1)} async-done(((bf16[48,1024]{1,0:T(8,128)(2,1)}), bf16[1536,1024]{1,0:T(8,128)(2,1)}) %all-gather.3.cloned.1.call-update) | async-done | bytes 3145744 | tf_op jit(solution)/shard_map/all_gather | solution.py:104
  138.1 4.1 %fusion.36 = f32[1536,256]{1,0:T(8,128)} fusion(bf16[1536,1024]{1,0:T(8,128)(2,1)} %all-gather.3.cloned.1.call-done, bf16[1024,256]{1,0:T(8,128)(2,1)S(1)} %copy-done), kind=kOutput, calls=%fused_computation.66 | convolution fusion | flops 805306368 | bytes 5242880 | tf_op jit(solution)/shard_map/dot_general | solution.py:103
  142.2 3.2 %bitcast_dynamic-update-slice_fusion.1 = (bf16[5,32,256]{2,1,0:T(8,128)(2,1)S(1)}, bf16[32,256]{1,0:T(8,128)(2,1)S(1)}) fusion(bf16[5,32,256]{2,1,0:T(8,128)(2,1)S(1)} %get-tuple-element.14, bf16[32,32,256]{2,1,0:T(8,128)(2,1)S(1)} %all-to-all-done.4, bf16[32,256,256]{2,1,0:T(8,128)(2,1)} %bitcast.132), kind=kOutput, calls=%fused_computation.53 | convolution fusion | flops 134234112 | bytes 4751360 | tf_op jit(solution)/shard_map/jwk,jkn->wn/dot_general | solution.py:121
  145.5 24.1 %all_to_all.37 = bf16[32,32,256]{2,1,0:T(8,128)(2,1)S(1)} all-to-all(bf16[32,32,256]{2,1,0:T(8,128)(2,1)S(1)} %broadcast_in_dim.108), channel_id=1, replica_groups=mesh['dp'=32,'tensor'=8] {'dp'}, dimensions={0} | all-to-all | bytes 1048576 | tf_op jit(solution)/shard_map/all_to_all | solution.py:12
  169.6 0.8 bitcast_dynamic-update-slice_fusion
  170.4 0.9 broadcast_in_dim.109
  171.3 4.8 %all-to-all-start.6 = ((bf16[32,32,256]{2,1,0:T(8,128)(2,1)}), bf16[32,32,256]{2,1,0:T(8,128)(2,1)S(1)}, u32[]{:S(2)}, u32[]{:S(2)}) async-start(bf16[32,32,256]{2,1,0:T(8,128)(2,1)} %broadcast_in_dim.109), calls=%async_computation.7 | async-start | bytes 1048576 | tf_op jit(solution)/shard_map/all_to_all | solution.py:12
  176.5 0.9 add_convert_fusion
  177.5 0.7 copy.25
  178.1 14.5 %all-to-all-done.6 = bf16[32,32,256]{2,1,0:T(8,128)(2,1)S(1)} async-done(((bf16[32,32,256]{2,1,0:T(8,128)(2,1)}), bf16[32,32,256]{2,1,0:T(8,128)(2,1)S(1)}, u32[]{:S(2)}, u32[]{:S(2)}) %all-to-all-start.6) | async-done | bytes 524320 | tf_op jit(solution)/shard_map/all_to_all | solution.py:12
  192.7 3.0 %fusion.22 = bf16[5,32,256]{2,1,0:T(8,128)(2,1)S(1)} fusion(bf16[5,32,256]{2,1,0:T(8,128)(2,1)S(1)} %get-tuple-element.18, bf16[32,32,256]{2,1,0:T(8,128)(2,1)S(1)} %all-to-all-done.6, bf16[32,256,256]{2,1,0:T(8,128)(2,1)} %bitcast.133), kind=kOutput, calls=%fused_computation.31 | convolution fusion | flops 134234112 | bytes 4734976 | tf_op jit(solution)/shard_map/jwk,jkn->wn/dot_general | solution.py:121
  195.7 0.6 copy-done.4
  (38 shorter events, 1.4 us)
Async XLA Ops:
  7.2 43.9 %copy-start = (bf16[1024,256]{1,0:T(8,128)(2,1)S(1)}, bf16[1024,256]{1,0:T(8,128)(2,1)}, u32[]{:S(2)}) copy-start(bf16[1024,256]{1,0:T(8,128)(2,1)} %param.18) | copy-start | bytes 1572868
  7.2 28.9 %copy-start.5 = (s32[32]{0:T(128)S(1)}, s32[32]{0:T(128)}, u32[]{:S(2)}) copy-start(s32[32]{0:T(128)} %param.16) | copy-start | bytes 388
  7.2 48.2 %copy-start.3 = (bf16[32,6,256]{2,0,1:T(8,128)(2,1)S(1)}, bf16[32,6,256]{2,0,1:T(8,128)(2,1)}, u32[]{:S(2)}) copy-start(bf16[32,6,256]{2,0,1:T(8,128)(2,1)} %param.17) | copy-start | bytes 294916
  7.2 78.2 %all-gather.5.cloned.1.call-start = ((), (), s32[]{:S(2)}) async-start(), calls=%async_computation.10 | async-start | bytes 4718592 | tf_op jit(solution)/shard_map/all_gather | solution.py:53
  7.9 130.1 %all-gather.3.cloned.1.call-start = ((), (), s32[]{:S(2)}) async-start(), calls=%async_computation.8 | async-start | bytes 3244032 | tf_op jit(solution)/shard_map/all_gather | solution.py:104
  8.0 6.0 %collective-permute-start = (s32[32]{0:T(128)}, s32[32]{0:T(128)S(1)}, u32[]{:S(2)}, u32[]{:S(2)}) collective-permute-start(s32[32]{0:T(128)} %param.16), channel_id=1, source_target_pairs={{0,0},{32,1},{64,2},{96,3},{128,4},{160,5},{192,6},{224,7},{8,8},{... | collective-permute-start | bytes 392 | tf_op jit(solution)/shard_map/ppermute | solution.py:23
  16.9 34.2 %all-to-all-start = ((bf16[32,8,1024]{2,1,0:T(8,128)(2,1)}), bf16[32,8,1024]{2,1,0:T(8,128)(2,1)S(1)}, u32[]{:S(2)}, u32[]{:S(2)}) async-start(bf16[32,8,1024]{2,1,0:T(8,128)(2,1)} %broadcast_in_dim.104), calls=%async_computation.1 | async-start | bytes 1048576 | tf_op jit(solution)/shard_map/all_to_all | solution.py:12
  52.0 9.4 %all-to-all-start.1 = ((bf16[8,32,256]{2,1,0:T(8,128)(2,1)}), bf16[8,32,256]{2,1,0:T(8,128)(2,1)S(1)}, u32[]{:S(2)}, u32[]{:S(2)}) async-start(bf16[8,32,256]{2,1,0:T(8,128)(2,1)} %bitcast.19), calls=%async_computation.2 | async-start | bytes 262144 | tf_op jit(solution)/shard_map/all_to_all | solution.py:93
  85.4 26.5 %copy-start.1 = (bf16[8192,256]{1,0:T(8,128)(2,1)S(1)}, bf16[8192,256]{1,0:T(8,128)(2,1)}, u32[]{:S(2)}) copy-start(bf16[8192,256]{1,0:T(8,128)(2,1)} %all-gather.5.cloned.1.call-done) | copy-start | bytes 12582916
  113.6 28.6 %all-to-all-start.4 = ((bf16[32,32,256]{2,1,0:T(8,128)(2,1)}), bf16[32,32,256]{2,1,0:T(8,128)(2,1)S(1)}, u32[]{:S(2)}, u32[]{:S(2)}) async-start(bf16[32,32,256]{2,1,0:T(8,128)(2,1)} %broadcast_in_dim.107), calls=%async_computation.5 | async-start | bytes 1048576 | tf_op jit(solution)/shard_map/all_to_all | solution.py:12
  119.1 57.4 %reduce-scatter.2.cloned.1.call-start = ((), (), s32[]{:S(2)}) async-start(), calls=%async_computation.9 | async-start | bytes 1769472 | tf_op jit(solution)/shard_map/reduce_scatter | solution.py:110
  142.2 27.4 %copy-start.2 = (bf16[8192,256]{1,0:T(8,128)(2,1)S(1)}, bf16[8192,256]{1,0:T(8,128)(2,1)}, u32[]{:S(2)}) copy-start(bf16[8192,256]{1,0:T(8,128)(2,1)} %all-gather.5.cloned.1.call-done) | copy-start | bytes 12582916
  171.3 21.4 %all-to-all-start.6 = ((bf16[32,32,256]{2,1,0:T(8,128)(2,1)}), bf16[32,32,256]{2,1,0:T(8,128)(2,1)S(1)}, u32[]{:S(2)}, u32[]{:S(2)}) async-start(bf16[32,32,256]{2,1,0:T(8,128)(2,1)} %broadcast_in_dim.109), calls=%async_computation.7 | async-start | bytes 1048576 | tf_op jit(solution)/shard_map/all_to_all | solution.py:12
  195.7 0.6 copy-start.4
Sparse Core Ops, SparseCore 0:
  9.9 37.2 all-gather.4
  50.4 87.6 all-gather.2
  142.3 34.1 reduce-scatter.1
where the time goes:
time: 204 us; the launch traced here: 203 us
  blocking collectives  71.2 us (35%)
  waiting for transfers between devices  55.3 us (27%)
  starting transfers between devices  34.3 us (17%)
  matrix products  20.8 us (10%)
  between operations  14 us (7%)
  local copies, waits for them, and re-layouts  4.89 us (2%)
  other arithmetic  2.43 us (1%)
    all_to_all x3, blocking collectives, spread(): return lax.all_to_all(copies, axis, split_axis=0, concat_axis=0, tiled=True)  71.2 us
    all_to_all x3, waiting for transfers between devices, spread(): return lax.all_to_all(copies, axis, split_axis=0, concat_axis=0, tiled=True)  29.5 us
    all_to_all x3, starting transfers between devices, spread(): return lax.all_to_all(copies, axis, split_axis=0, concat_axis=0, tiled=True)  29.5 us
    all_gather x1, waiting for transfers between devices, per_device(): lax.all_gather(attended.reshape(windows_here * tokens_here, query_width),...  18.9 us
    dot_general x5, matrix products, per_device(): jnp.einsum('jwk,jkn->wn', inputs, columns, preferred_element_type=jnp.flo...  11 us
    all_to_all x1, waiting for transfers between devices, per_device(): lax.all_to_all(picked_part.astype(jnp.bfloat16).reshape(tensor_size, bloc...  5.94 us
    dot_general x1, matrix products, per_device(): jnp.dot(lax.all_gather(attended.reshape(windows_here * tokens_here, query...  4.12 us
  transfers between devices with their start and end apart: 8, of which 5 were waited for; matrix products, arithmetic and copies ran while one was open for 12% of the time, Pallas kernels for 0%

commit v1 on v0

--- a/solution.py
+++ b/solution.py
@@ -1,3 +1,4 @@
+import functools
 import jax
 import jax.numpy as jnp
 from jax import lax
@@ -5,6 +6,20 @@
 
 HD = 128
 STEPS = 5
+
+
+def view_the_trails(sheet, ndim_at):
+    current_block = lax.all_to_all(
+        jnp.concatenate([sheet] * lax.axis_size("dp"), axis=ndim_at),
+        "dp",
+        ndim_at,
+        ndim_at,
+        tiled=True,
+    )
+    return current_block
+
+
+touch_vectors = functools.partial(view_the_trails, ndim_at=0)
 
 
 def spread(block, axis):
@@ -101,9 +116,7 @@
         pick(residual, accepted).astype(jnp.float32) + jnp.sum(shares.astype(jnp.float32), axis=0)
     ).astype(jnp.bfloat16)
     partial_out = jnp.dot(
-        lax.all_gather(
-            attended.reshape(windows_here * tokens_here, query_width), "dp", axis=0, tiled=True
-        ),
+        touch_vectors(attended.reshape(windows_here * tokens_here, query_width)),
         out_weight,
         preferred_element_type=jnp.float32,
     )

time: 204 us -> 273 us (1.34)
  waiting for transfers between devices: 55.3 us -> 130 us
  blocking collectives: 71.2 us -> 21.5 us
  local copies, waits for them, and re-layouts: 4.89 us -> 26.5 us
  starting transfers between devices: 34.3 us -> 54.8 us
    all_to_all x0 -> x1, waiting for transfers between devices: none -> 67.2 us  [view_the_trails(): lax.all_to_all(jnp.concatenate([sheet] * lax.axis_size('dp'), axis=ndim_a...]
    all_to_all x3 -> x1, blocking collectives: 71.2 us -> 21.5 us  [spread(): return lax.all_to_all(copies, axis, split_axis=0, concat_axis=0, tiled=True)]
    all_to_all x3 -> x5, waiting for transfers between devices: 29.5 us -> 57.6 us  [spread(): return lax.all_to_all(copies, axis, split_axis=0, concat_axis=0, tiled=True)]
    unnamed x15 -> x45, local copies, waits for them, and re-layouts: 1.98 us -> 21.4 us
    all_gather x1 -> x0, waiting for transfers between devices: 18.9 us -> none  [per_device(): lax.all_gather(attended.reshape(windows_here * tokens_here, query_width),...]
    all_to_all x3 -> x5, starting transfers between devices: 29.5 us -> 45 us  [spread(): return lax.all_to_all(copies, axis, split_axis=0, concat_axis=0, tiled=True)]
    all_to_all x0 -> x1, starting transfers between devices: none -> 4.91 us  [view_the_trails(): lax.all_to_all(jnp.concatenate([sheet] * lax.axis_size('dp'), axis=ndim_a...]
  transfers between devices with their start and end apart: 8 -> 10, of which waited for: 5 -> 7; matrix products, arithmetic and copies ran while one was open for 12% -> 16% of each run, Pallas kernels for 0% -> 0%
where the time goes in v1:
time: 273 us; the launch traced here: 272 us
  waiting for transfers between devices  130 us (48%)
  starting transfers between devices  54.8 us (20%)
  local copies, waits for them, and re-layouts  26.5 us (10%)
  blocking collectives  21.5 us (8%)
  matrix products  21.1 us (8%)
  between operations  14.4 us (5%)
  other arithmetic  3.09 us (1%)
    all_to_all x1, waiting for transfers between devices, view_the_trails(): lax.all_to_all(jnp.concatenate([sheet] * lax.axis_size('dp'), axis=ndim_a...  67.2 us
    all_to_all x5, waiting for transfers between devices, spread(): return lax.all_to_all(copies, axis, split_axis=0, concat_axis=0, tiled=True)  57.6 us
    all_to_all x5, starting transfers between devices, spread(): return lax.all_to_all(copies, axis, split_axis=0, concat_axis=0, tiled=True)  45 us
    all_to_all x1, blocking collectives, spread(): return lax.all_to_all(copies, axis, split_axis=0, concat_axis=0, tiled=True)  21.5 us
    unnamed x45, local copies, waits for them, and re-layouts  21.4 us
    dot_general x5, matrix products, per_device(): jnp.einsum('jwk,jkn->wn', inputs, columns, preferred_element_type=jnp.flo...  13.1 us
  transfers between devices with their start and end apart: 10, of which 7 were waited for; matrix products, arithmetic and copies ran while one was open for 16% of the time, Pallas kernels for 0%

profile of v1, /device:TPU:32, one launch (start us, length us, event | category | flops | bytes accessed | tf_op | source)
XLA Modules:
  0.0 271.6 jit_solution(5033261812633513819)
XLA Ops:
  7.3 1.4 collective-permute-start
  9.4 0.7 iota_compare_fusion
  10.1 1.4 fusion.34
  11.6 1.2 fusion.35
  13.9 0.8 broadcast_in_dim.104
  14.8 18.9 %all-to-all-start.1 = ((bf16[32,8,1024]{2,1,0:T(8,128)(2,1)}), bf16[32,8,1024]{2,1,0:T(8,128)(2,1)S(1)}, u32[]{:S(2)}, u32[]{:S(2)}) async-start(bf16[32,8,1024]{2,1,0:T(8,128)(2,1)} %broadcast_in_dim.104), calls=%async_computation.2 | async-start | bytes 1048576 | tf_op jit(solution)/shard_map/all_to_all | solution.py:27
  47.3 1.5 all-to-all-done.1
  48.8 0.9 convolution_convert_fusion
  49.8 3.4 %all-to-all-start.2 = ((bf16[8,32,256]{2,1,0:T(8,128)(2,1)}), bf16[8,32,256]{2,1,0:T(8,128)(2,1)S(1)}, u32[]{:S(2)}, u32[]{:S(2)}) async-start(bf16[8,32,256]{2,1,0:T(8,128)(2,1)} %bitcast.21), calls=%async_computation.3 | async-start | bytes 262144 | tf_op jit(solution)/shard_map/all_to_all | solution.py:108
  53.8 5.4 %all-to-all-done.2 = bf16[8,32,256]{2,1,0:T(8,128)(2,1)S(1)} async-done(((bf16[8,32,256]{2,1,0:T(8,128)(2,1)}), bf16[8,32,256]{2,1,0:T(8,128)(2,1)S(1)}, u32[]{:S(2)}, u32[]{:S(2)}) %all-to-all-start.2) | async-done | bytes 131104 | tf_op jit(solution)/shard_map/all_to_all | solution.py:108
  59.2 0.8 broadcast_in_dim.105
  60.1 8.3 %all-to-all-start.3 = ((bf16[32,32,256]{2,1,0:T(8,128)(2,1)}), bf16[32,32,256]{2,1,0:T(8,128)(2,1)S(1)}, u32[]{:S(2)}, u32[]{:S(2)}) async-start(bf16[32,32,256]{2,1,0:T(8,128)(2,1)} %broadcast_in_dim.105), calls=%async_computation.4 | async-start | bytes 1048576 | tf_op jit(solution)/shard_map/all_to_all | solution.py:27
  71.6 14.2 %all-to-all-done.3 = bf16[32,32,256]{2,1,0:T(8,128)(2,1)S(1)} async-done(((bf16[32,32,256]{2,1,0:T(8,128)(2,1)}), bf16[32,32,256]{2,1,0:T(8,128)(2,1)S(1)}, u32[]{:S(2)}, u32[]{:S(2)}) %all-to-all-start.3) | async-done | bytes 524320 | tf_op jit(solution)/shard_map/all_to_all | solution.py:27
  85.8 3.0 %constant_dynamic-update-slice_fusion.3 = (bf16[5,32,256]{2,1,0:T(8,128)(2,1)S(1)}, bf16[32,256]{1,0:T(8,128)(2,1)S(1)}) fusion(bf16[32,32,256]{2,1,0:T(8,128)(2,1)S(1)} %all-to-all-done.3, bf16[32,256,256]{2,1,0:T(8,128)(2,1)} %bitcast.195), kind=kOutput, calls=%fused_computation.84 | convolution fusion | flops 134234112 | bytes 4751360 | tf_op jit(solution)/shard_map/jwk,jkn->wn/dot_general | solution.py:134
  88.8 0.8 broadcast_in_dim.106
  89.7 4.8 %all-to-all-start.4 = ((bf16[32,32,256]{2,1,0:T(8,128)(2,1)}), bf16[32,32,256]{2,1,0:T(8,128)(2,1)S(1)}, u32[]{:S(2)}, u32[]{:S(2)}) async-start(bf16[32,32,256]{2,1,0:T(8,128)(2,1)} %broadcast_in_dim.106), calls=%async_computation.5 | async-start | bytes 1048576 | tf_op jit(solution)/shard_map/all_to_all | solution.py:27
  97.8 13.7 %all-to-all-done.4 = bf16[32,32,256]{2,1,0:T(8,128)(2,1)S(1)} async-done(((bf16[32,32,256]{2,1,0:T(8,128)(2,1)}), bf16[32,32,256]{2,1,0:T(8,128)(2,1)S(1)}, u32[]{:S(2)}, u32[]{:S(2)}) %all-to-all-start.4) | async-done | bytes 524320 | tf_op jit(solution)/shard_map/all_to_all | solution.py:27
  111.5 4.9 %all-to-all-start = ((bf16[32,48,1024]{2,1,0:T(8,128)(2,1)}), bf16[32,48,1024]{2,1,0:T(8,128)(2,1)}, u32[]{:S(2)}, u32[]{:S(2)}) async-start(bf16[32,48,1024]{2,1,0:T(8,128)(2,1)} %bitcast.16), calls=%async_computation | async-start | bytes 6291456 | tf_op jit(solution)/shard_map/all_to_all | solution.py:12
  116.4 3.0 %constant_dynamic-update-slice_fusion.2 = (bf16[5,32,256]{2,1,0:T(8,128)(2,1)S(1)}, bf16[32,256]{1,0:T(8,128)(2,1)S(1)}) fusion(bf16[5,32,256]{2,1,0:T(8,128)(2,1)S(1)} %get-tuple-element.12, bf16[32,32,256]{2,1,0:T(8,128)(2,1)S(1)} %all-to-all-done.4, bf16[32,256,256]{2,1,0:T(8,128)(2,1)} %bitcast.196), kind=kOutput, calls=%fused_computation.83 | convolution fusion | flops 134234112 | bytes 4751360 | tf_op jit(solution)/shard_map/jwk,jkn->wn/dot_general | solution.py:134
  119.4 67.2 %all-to-all-done = bf16[32,48,1024]{2,1,0:T(8,128)(2,1)} async-done(((bf16[32,48,1024]{2,1,0:T(8,128)(2,1)}), bf16[32,48,1024]{2,1,0:T(8,128)(2,1)}, u32[]{:S(2)}, u32[]{:S(2)}) %all-to-all-start) | async-done | bytes 3145760 | tf_op jit(solution)/shard_map/all_to_all | solution.py:12
  186.6 0.9 broadcast_in_dim.107
  187.5 8.0 %all-to-all-start.5 = ((bf16[32,32,256]{2,1,0:T(8,128)(2,1)}), bf16[32,32,256]{2,1,0:T(8,128)(2,1)S(1)}, u32[]{:S(2)}, u32[]{:S(2)}) async-start(bf16[32,32,256]{2,1,0:T(8,128)(2,1)} %broadcast_in_dim.107), calls=%async_computation.6 | async-start | bytes 1048576 | tf_op jit(solution)/shard_map/all_to_all | solution.py:27
  195.6 4.1 %fusion.36 = f32[1536,256]{1,0:T(8,128)} fusion(bf16[1536,1024]{1,0:T(8,128)(2,1)} %bitcast.17, bf16[1024,256]{1,0:T(8,128)(2,1)S(1)} %copy-done), kind=kOutput, calls=%fused_computation.97 | convolution fusion | flops 805306368 | bytes 5242880 | tf_op jit(solution)/shard_map/dot_general | solution.py:118
  199.7 13.3 %all-to-all-done.5 = bf16[32,32,256]{2,1,0:T(8,128)(2,1)S(1)} async-done(((bf16[32,32,256]{2,1,0:T(8,128)(2,1)}), bf16[32,32,256]{2,1,0:T(8,128)(2,1)S(1)}, u32[]{:S(2)}, u32[]{:S(2)}) %all-to-all-start.5) | async-done | bytes 524320 | tf_op jit(solution)/shard_map/all_to_all | solution.py:27
  213.0 3.2 %constant_dynamic-update-slice_fusion.1 = (bf16[5,32,256]{2,1,0:T(8,128)(2,1)S(1)}, bf16[32,256]{1,0:T(8,128)(2,1)S(1)}) fusion(bf16[5,32,256]{2,1,0:T(8,128)(2,1)S(1)} %get-tuple-element.14, bf16[32,32,256]{2,1,0:T(8,128)(2,1)S(1)} %all-to-all-done.5, bf16[32,256,256]{2,1,0:T(8,128)(2,1)} %bitcast.197), kind=kOutput, calls=%fused_computation.82 | convolution fusion | flops 134234112 | bytes 4751360 | tf_op jit(solution)/shard_map/jwk,jkn->wn/dot_general | solution.py:134
  216.3 21.5 %all_to_all.47 = bf16[32,32,256]{2,1,0:T(8,128)(2,1)S(1)} all-to-all(bf16[32,32,256]{2,1,0:T(8,128)(2,1)S(1)} %broadcast_in_dim.108), channel_id=1, replica_groups=mesh['dp'=32,'tensor'=8] {'dp'}, dimensions={0} | all-to-all | bytes 1048576 | tf_op jit(solution)/shard_map/all_to_all | solution.py:27
  237.8 0.8 constant_dynamic-update-slice_fusion
  238.6 0.8 broadcast_in_dim.109
  239.5 4.9 %all-to-all-start.7 = ((bf16[32,32,256]{2,1,0:T(8,128)(2,1)}), bf16[32,32,256]{2,1,0:T(8,128)(2,1)S(1)}, u32[]{:S(2)}, u32[]{:S(2)}) async-start(bf16[32,32,256]{2,1,0:T(8,128)(2,1)} %broadcast_in_dim.109), calls=%async_computation.8 | async-start | bytes 1048576 | tf_op jit(solution)/shard_map/all_to_all | solution.py:27
  244.5 0.9 add_convert_fusion
  246.1 15.0 %all-to-all-done.7 = bf16[32,32,256]{2,1,0:T(8,128)(2,1)S(1)} async-done(((bf16[32,32,256]{2,1,0:T(8,128)(2,1)}), bf16[32,32,256]{2,1,0:T(8,128)(2,1)S(1)}, u32[]{:S(2)}, u32[]{:S(2)}) %all-to-all-start.7) | async-done | bytes 524320 | tf_op jit(solution)/shard_map/all_to_all | solution.py:27
  261.1 3.0 %fusion.22 = bf16[5,32,256]{2,1,0:T(8,128)(2,1)S(1)} fusion(bf16[5,32,256]{2,1,0:T(8,128)(2,1)S(1)} %get-tuple-element.18, bf16[32,32,256]{2,1,0:T(8,128)(2,1)S(1)} %all-to-all-done.7, bf16[32,256,256]{2,1,0:T(8,128)(2,1)} %bitcast.198), kind=kOutput, calls=%fused_computation.31 | convolution fusion | flops 134234112 | bytes 4734976 | tf_op jit(solution)/shard_map/jwk,jkn->wn/dot_general | solution.py:134
  (70 shorter events, 24.1 us)
Async XLA Ops:
  7.2 41.6 %copy-start = (bf16[1024,256]{1,0:T(8,128)(2,1)S(1)}, bf16[1024,256]{1,0:T(8,128)(2,1)}, u32[]{:S(2)}) copy-start(bf16[1024,256]{1,0:T(8,128)(2,1)} %param.18) | copy-start | bytes 1572868
  7.2 6.0 %copy-start.4 = (bf16[8,6,128]{2,0,1:T(8,128)(2,1)S(1)}, bf16[8,6,128]{2,0,1:T(8,128)(2,1)}, u32[]{:S(2)}) copy-start(bf16[8,6,128]{2,0,1:T(8,128)(2,1)} %param.12) | copy-start | bytes 36868
  7.2 6.2 %copy-start.3 = (bf16[32,6,256]{2,0,1:T(8,128)(2,1)S(1)}, bf16[32,6,256]{2,0,1:T(8,128)(2,1)}, u32[]{:S(2)}) copy-start(bf16[32,6,256]{2,0,1:T(8,128)(2,1)} %param.17) | copy-start | bytes 294916
  7.2 6.5 %copy-start.2 = (bf16[8,256,128]{2,1,0:T(8,128)(2,1)S(1)}, bf16[8,256,128]{2,1,0:T(8,128)(2,1)}, u32[]{:S(2)}) copy-start(bf16[8,256,128]{2,1,0:T(8,128)(2,1)} %param.14) | copy-start | bytes 1572868
  7.2 78.6 %all-gather.2.cloned.1.call-start = ((), (), s32[]{:S(2)}) async-start(), calls=%async_computation.10 | async-start | bytes 4718592 | tf_op jit(solution)/shard_map/all_gather | solution.py:68
  7.3 6.2 %collective-permute-start = (s32[32]{0:T(128)}, s32[32]{0:T(128)S(1)}, u32[]{:S(2)}, u32[]{:S(2)}) collective-permute-start(s32[32]{0:T(128)} %param.16), channel_id=1, source_target_pairs={{0,0},{32,1},{64,2},{96,3},{128,4},{160,5},{192,6},{224,7},{8,8},{... | collective-permute-start | bytes 392 | tf_op jit(solution)/shard_map/ppermute | solution.py:38
  14.8 34.0 %all-to-all-start.1 = ((bf16[32,8,1024]{2,1,0:T(8,128)(2,1)}), bf16[32,8,1024]{2,1,0:T(8,128)(2,1)S(1)}, u32[]{:S(2)}, u32[]{:S(2)}) async-start(bf16[32,8,1024]{2,1,0:T(8,128)(2,1)} %broadcast_in_dim.104), calls=%async_computation.2 | async-start | bytes 1048576 | tf_op jit(solution)/shard_map/all_to_all | solution.py:27
  49.8 9.4 %all-to-all-start.2 = ((bf16[8,32,256]{2,1,0:T(8,128)(2,1)}), bf16[8,32,256]{2,1,0:T(8,128)(2,1)S(1)}, u32[]{:S(2)}, u32[]{:S(2)}) async-start(bf16[8,32,256]{2,1,0:T(8,128)(2,1)} %bitcast.21), calls=%async_computation.3 | async-start | bytes 262144 | tf_op jit(solution)/shard_map/all_to_all | solution.py:108
  60.1 25.8 %all-to-all-start.3 = ((bf16[32,32,256]{2,1,0:T(8,128)(2,1)}), bf16[32,32,256]{2,1,0:T(8,128)(2,1)S(1)}, u32[]{:S(2)}, u32[]{:S(2)}) async-start(bf16[32,32,256]{2,1,0:T(8,128)(2,1)} %broadcast_in_dim.105), calls=%async_computation.4 | async-start | bytes 1048576 | tf_op jit(solution)/shard_map/all_to_all | solution.py:27
  89.7 21.8 %all-to-all-start.4 = ((bf16[32,32,256]{2,1,0:T(8,128)(2,1)}), bf16[32,32,256]{2,1,0:T(8,128)(2,1)S(1)}, u32[]{:S(2)}, u32[]{:S(2)}) async-start(bf16[32,32,256]{2,1,0:T(8,128)(2,1)} %broadcast_in_dim.106), calls=%async_computation.5 | async-start | bytes 1048576 | tf_op jit(solution)/shard_map/all_to_all | solution.py:27
  111.5 75.1 %all-to-all-start = ((bf16[32,48,1024]{2,1,0:T(8,128)(2,1)}), bf16[32,48,1024]{2,1,0:T(8,128)(2,1)}, u32[]{:S(2)}, u32[]{:S(2)}) async-start(bf16[32,48,1024]{2,1,0:T(8,128)(2,1)} %bitcast.16), calls=%async_computation | async-start | bytes 6291456 | tf_op jit(solution)/shard_map/all_to_all | solution.py:12
  187.5 25.5 %all-to-all-start.5 = ((bf16[32,32,256]{2,1,0:T(8,128)(2,1)}), bf16[32,32,256]{2,1,0:T(8,128)(2,1)S(1)}, u32[]{:S(2)}, u32[]{:S(2)}) async-start(bf16[32,32,256]{2,1,0:T(8,128)(2,1)} %broadcast_in_dim.107), calls=%async_computation.6 | async-start | bytes 1048576 | tf_op jit(solution)/shard_map/all_to_all | solution.py:27
  195.5 49.0 %reduce-scatter.2.cloned.1.call-start = ((), (), s32[]{:S(2)}) async-start(), calls=%async_computation.9 | async-start | bytes 1769472 | tf_op jit(solution)/shard_map/reduce_scatter | solution.py:123
  213.0 24.8 %copy-start.1 = (bf16[8192,256]{1,0:T(8,128)(2,1)S(1)}, bf16[8192,256]{1,0:T(8,128)(2,1)}, u32[]{:S(2)}) copy-start(bf16[8192,256]{1,0:T(8,128)(2,1)} %all-gather.2.cloned.1.call-done) | copy-start | bytes 12582916
  239.5 21.6 %all-to-all-start.7 = ((bf16[32,32,256]{2,1,0:T(8,128)(2,1)}), bf16[32,32,256]{2,1,0:T(8,128)(2,1)S(1)}, u32[]{:S(2)}, u32[]{:S(2)}) async-start(bf16[32,32,256]{2,1,0:T(8,128)(2,1)} %broadcast_in_dim.109), calls=%async_computation.8 | async-start | bytes 1048576 | tf_op jit(solution)/shard_map/all_to_all | solution.py:27
  264.1 0.6 copy-start.5
Sparse Core Ops, SparseCore 0:
  9.9 39.2 all-gather.1
  199.8 34.5 reduce-scatter.1
